TPU v7x, 256 devices: a whole 4x4x8 slice. The times are simulated.
256 devices in a mesh: freq: 32 (over y_hi, z, core), tm: 4 (over x), grp: 2 (over y_lo).
Axes of the slice: x: 4, y: 4 (y_hi: 2, y_lo: 2; y = y_hi * 2 + y_lo), z: 8, core: 2. Of those that a mesh axis runs over, the one named last changes fastest.
Arguments:
- voltages: bfloat16 [32, 2, 1024, 4096], P(None, None, ('freq', 'grp'), 'tm'), may hold values from -6 to 6
- prior_gains: float32 [32, 2, 1024], P('freq'), may hold values from -4.2 to 4.2
- station_flags: int32 [512], replicated, may hold values 0 or 1
- ingest_map: int32 [512], replicated, may hold values from 0 to 511, each once
- station_coords: float32 [2, 512], replicated, may hold values from -40 to 40
- pointing: int32 [2, 256], replicated, may hold values from 0 to 63
- corr_channels: int32 [32], replicated, may hold values from 0 to 31, each once
- beam_channels: int32 [32], replicated, may hold values from 0 to 31, each once
Outputs:
- visibilities: float32 [32, 2, 1024, 1024], P('freq', None, 'grp', 'tm')
- solved_gains: float32 [32, 2, 1024], P('freq')
- tied_beams: bfloat16 [32, 2, 2, 256, 4096], P('freq', None, None, 'grp', 'tm')
Inputs may be any that keep to these rules, and one draw needn't show every extreme that they name: `ingest_map`: each station appears in exactly one ingest slot. `corr_channels`: each channel is handled by exactly one correlator slot. `beam_channels`: each channel is handled by exactly one beamformer slot.
All inputs are finite; a program needn't handle non-finite values.
Results may differ from a plain program's by a relative error of at most 0.0049.
Values may be sent and summed in bfloat16 or wider, within the bound.
No kernel may reach another device: no remote copies, remote signals or barrier semaphores. Data moves between devices by JAX's collectives and lax.ppermute only.
A program may use at most 64 MiB of HBM per device.

v0:
```python
import math
import jax
import jax.numpy as jnp
from jax import lax
from jax.sharding import PartitionSpec as P

S = 512
ITERS = 4
grid_cells = 64.0


def weights_for(gains_sel, ratio, pointing_part, slot_coords):
    east_dir = (pointing_part[0].astype(jnp.float32) + 0.5) / grid_cells - 0.5
    north_dir = (pointing_part[1].astype(jnp.float32) + 0.5) / grid_cells - 0.5
    phase = (
        2.0
        * math.pi
        * ratio
        * (
            east_dir[:, None] * slot_coords[0][None, :]
            + north_dir[:, None] * slot_coords[1][None, :]
        )
    )
    cosine = jnp.cos(phase)
    sine = jnp.sin(phase)
    gain_real = gains_sel[0].reshape(2, S)
    gain_imag = gains_sel[1].reshape(2, S)
    denom = jnp.maximum(gain_real * gain_real + gain_imag * gain_imag, 0.5)
    along_real = gain_real / denom
    along_imag = gain_imag / denom
    factor = 1.0 / math.sqrt(S)
    w_real = (cosine[None] * along_real[:, None, :] - sine[None] * along_imag[:, None, :]) * factor
    w_imag = -(cosine[None] * along_imag[:, None, :] + sine[None] * along_real[:, None, :]) * factor
    upper = jnp.stack([w_real, -w_imag], axis=2)
    lower = jnp.stack([w_imag, w_real], axis=2)
    return jnp.stack([upper, lower], axis=1).astype(jnp.bfloat16)


def body(
    voltages,
    prior_gains,
    station_flags,
    ingest_map,
    station_coords,
    pointing,
    corr_channels,
    beam_channels,
):
    highest = lax.Precision.HIGHEST
    n_freq = lax.axis_size("freq")
    n_time = lax.axis_size("tm")
    n_group = lax.axis_size("grp")
    freq_index = lax.axis_index("freq")
    time_index = lax.axis_index("tm")
    group_index = lax.axis_index("grp")
    channels_all = voltages.shape[0]
    per_device = channels_all // n_freq
    samples = voltages.shape[3]
    inputs_all = 2 * S
    paired = lax.all_gather(voltages, "grp", axis=2, tiled=True)
    corr_source = jnp.take(paired, corr_channels, axis=0)
    beam_source = jnp.take(paired, beam_channels, axis=0)
    corr_volts, beam_volts = (
        lax.all_to_all(corr_source, "freq", split_axis=0, concat_axis=2, tiled=True),
        lax.all_to_all(beam_source, "freq", split_axis=0, concat_axis=2, tiled=True),
    )
    slot_keep = 1 - jnp.take(station_flags, ingest_map)
    keep = jnp.concatenate([slot_keep, slot_keep]).astype(jnp.bfloat16)
    corr_volts = corr_volts * keep[None, None, :, None]
    beam_volts = beam_volts * keep[None, None, :, None]
    rows = inputs_all // n_group
    row_start = group_index * rows
    mine = lax.dynamic_slice_in_dim(corr_volts, row_start, rows, 2)
    left = jnp.stack([mine, jnp.stack([mine[:, 1], -mine[:, 0]], axis=1)], axis=1)
    partial_value = jnp.einsum(
        "corit,crjt->coij", left, corr_volts, preferred_element_type=jnp.float32
    )
    partial_value = partial_value * (1.0 / (samples * n_time))
    columns = inputs_all // n_time
    vis_block = lax.psum_scatter(partial_value, "tm", scatter_dimension=3, tiled=True)
    gains = prior_gains
    for iteration in range(ITERS):
        power = jnp.sum(gains * gains, axis=(1, 2)) + 1e-06
        along = lax.dynamic_slice_in_dim(gains, time_index * columns, columns, 2)
        real_real = jnp.einsum("cij,cj->ci", vis_block[:, 0], along[:, 0], precision=highest)
        imag_imag = jnp.einsum("cij,cj->ci", vis_block[:, 1], along[:, 1], precision=highest)
        real_imag = jnp.einsum("cij,cj->ci", vis_block[:, 0], along[:, 1], precision=highest)
        imag_real = jnp.einsum("cij,cj->ci", vis_block[:, 1], along[:, 0], precision=highest)
        update = jnp.stack([real_real - imag_imag, imag_real + real_imag], axis=1)
        update = lax.psum(update, "tm")
        own_rows = lax.dynamic_slice_in_dim(gains, row_start, rows, 2)
        fresh = 0.5 * (own_rows + inputs_all * update / power[:, None, None])
        gains = lax.all_gather(fresh, "grp", axis=2, tiled=True)
    all_gains = lax.all_gather(gains, "freq", axis=0, tiled=True)
    my_beam = lax.dynamic_slice_in_dim(beam_channels, freq_index * per_device, per_device, 0)
    onehot = (corr_channels[None, :] == my_beam[:, None]).astype(jnp.float32)
    selected = jnp.einsum("ck,kri->cri", onehot, all_gains, precision=highest)
    ratio = 0.875 + 0.25 * (my_beam.astype(jnp.float32) + 0.5) / channels_all
    beams_mine = pointing.shape[1] // n_group
    pointing_part = lax.dynamic_slice_in_dim(pointing, group_index * beams_mine, beams_mine, 1)
    slot_coords = jnp.take(station_coords, ingest_map, axis=1)
    weights = jax.vmap(weights_for, in_axes=(0, 0, None, None))(
        selected, ratio, pointing_part, slot_coords
    )
    block = beam_volts.reshape(per_device, 2, 2, S, samples)
    beams = jnp.einsum("cpobrq,crpqt->cpobt", weights, block, preferred_element_type=jnp.float32)
    return (vis_block, gains, beams.astype(jnp.bfloat16))


def solution(mesh):
    return jax.shard_map(
        body,
        mesh=mesh,
        in_specs=(
            P(None, None, ("freq", "grp"), "tm"),
            P("freq", None, None),
            P(),
            P(),
            P(),
            P(),
            P(),
            P(),
        ),
        out_specs=(
            P("freq", None, "grp", "tm"),
            P("freq", None, None),
            P("freq", None, None, "grp", "tm"),
        ),
        check_vma=False,
    )
```

profile of v0, /device:TPU:1, one launch (start us, length us, event | category | flops | bytes accessed | tf_op | source)
XLA Modules:
  0.0 446.5 jit_solution(17262730501101874338)
XLA Ops:
  9.3 66.2 %all-gather.2.cloned.1.call-done = bf16[32,2,32,1024]{3,2,1,0:T(8,128)(2,1)} async-done(((bf16[32,2,16,1024]{3,2,1,0:T(8,128)(2,1)}), bf16[32,2,32,1024]{3,2,1,0:T(8,128)(2,1)}) %all-gather.2.cloned.1.call-update) | async-done | bytes 4194320 | tf_op jit(solution)/shard_map/all_gather | solution.py:60
  75.5 5.0 %gather_fusion.2 = bf16[32,2,32,1024]{3,2,1,0:T(8,128)(2,1)} fusion(bf16[32,2,32,1024]{3,2,1,0:T(8,128)(2,1)} %all-gather.2.cloned.1.call-done, s32[1024]{0:T(1024)S(1)} %pad_clamp_fusion.2), kind=kCustom, calls=%fused_computation.clone | custom fusion | bytes 8388736 | tf_op jit(solution)/shard_map/jit(_take)/gather | solution.py:61
  80.4 4.6 %broadcast_select_fusion.1 = bf16[32,2,32,1024]{3,2,1,0:T(8,128)(2,1)} fusion(bf16[32,2,32,1024]{3,2,1,0:T(8,128)(2,1)} %gather_fusion.2, pred[32]{0:T(512)(128)(4,1)S(1)} %get-tuple-element.27), kind=kLoop, calls=%fused_computation.14 | loop fusion | flops 2097152 | bytes 8388640 | tf_op jit(solution)/shard_map/jit(_take)/select_n | solution.py:61
  85.1 10.2 %all-to-all-start = ((bf16[32,2,32,1024]{3,2,1,0:T(8,128)(2,1)}), bf16[32,2,32,1024]{3,2,1,0:T(8,128)(2,1)}, u32[]{:S(2)}, u32[]{:S(2)}) async-start(bf16[32,2,32,1024]{3,2,1,0:T(8,128)(2,1)} %broadcast_select_fusion.1), calls=%async_computation | async-start | bytes 8388608 | tf_op jit(solution)/shard_map/all_to_all | solution.py:64
  95.3 3.5 gather_fusion
  99.1 5.0 %gather_fusion.3 = bf16[32,2,32,1024]{3,2,1,0:T(8,128)(2,1)} fusion(bf16[32,2,32,1024]{3,2,1,0:T(8,128)(2,1)} %all-gather.2.cloned.1.call-done, s32[1024]{0:T(1024)S(1)} %pad_clamp_fusion), kind=kCustom, calls=%fused_computation.1.clone | custom fusion | bytes 8388736 | tf_op jit(solution)/shard_map/jit(_take)/gather | solution.py:62
  104.1 87.4 %all-to-all-done = bf16[32,2,32,1024]{3,2,1,0:T(8,128)(2,1)} async-done(((bf16[32,2,32,1024]{3,2,1,0:T(8,128)(2,1)}), bf16[32,2,32,1024]{3,2,1,0:T(8,128)(2,1)}, u32[]{:S(2)}, u32[]{:S(2)}) %all-to-all-start) | async-done | bytes 4194336 | tf_op jit(solution)/shard_map/all_to_all | solution.py:64
  191.4 2.6 copy.23
  194.9 2.5 broadcast_multiply_fusion
  198.6 6.1 %fusion.5 = f32[1,2,512,1024]{3,2,1,0:T(8,128)} fusion(bf16[2,1024,1024,1]{2,1,0,3:T(8,128)(2,1)S(1)} %bitcast.170, bf16[1,1,2,512,1024]{4,3,2,1,0:T(8,128)(2,1)S(1)} %maximum_bitcast_fusion.4, bf16[1,1,2,512,1024]{4,3,2,1,0:T(8,128)(2,1)S(1)} %fusion.76), kind=kOutput, calls=%fused_computation.11 | convolution fusion | flops 4298113024 | bytes 12582912 | tf_op jit(solution)/shard_map/corit,crjt->coij/dot_general | solution.py:75
  204.7 4.6 %broadcast_select_fusion = bf16[32,2,32,1024]{3,2,1,0:T(8,128)(2,1)} fusion(bf16[32,2,32,1024]{3,2,1,0:T(8,128)(2,1)} %gather_fusion.3, pred[32]{0:T(512)(128)(4,1)S(1)} %get-tuple-element.26), kind=kLoop, calls=%fused_computation.13 | loop fusion | flops 2097152 | bytes 8388640 | tf_op jit(solution)/shard_map/jit(_take)/select_n | solution.py:62
  209.4 7.4 %all-to-all-start.1 = ((bf16[32,2,32,1024]{3,2,1,0:T(8,128)(2,1)}), bf16[32,2,32,1024]{3,2,1,0:T(8,128)(2,1)}, u32[]{:S(2)}, u32[]{:S(2)}) async-start(bf16[32,2,32,1024]{3,2,1,0:T(8,128)(2,1)} %broadcast_select_fusion), calls=%async_computation.2 | async-start | bytes 8388608 | tf_op jit(solution)/shard_map/all_to_all | solution.py:65
  222.1 90.9 %all-to-all-done.1 = bf16[32,2,32,1024]{3,2,1,0:T(8,128)(2,1)} async-done(((bf16[32,2,32,1024]{3,2,1,0:T(8,128)(2,1)}), bf16[32,2,32,1024]{3,2,1,0:T(8,128)(2,1)}, u32[]{:S(2)}, u32[]{:S(2)}) %all-to-all-start.1) | async-done | bytes 4194336 | tf_op jit(solution)/shard_map/all_to_all | solution.py:65
  313.0 5.0 %copy.27 = bf16[1,2,32,32,1024]{4,3,2,1,0:T(8,128)(2,1)} copy(bf16[1,2,32,32,1024]{4,3,1,2,0:T(8,128)(2,1)} %bitcast.74) | data formatting | bytes 8388608 | tf_op jit(solution)/shard_map/all_to_all | solution.py:65
  324.5 8.4 %psum.28 = f32[1,2,512]{2,1,0:T(2,128)S(1)} all-reduce(f32[1,2,512]{2,1,0:T(2,128)S(1)} %pad_maximum_fusion), channel_id=1, replica_groups=mesh['freq'=32,'tm'=4,'grp'=2] {'tm'}, use_global_device_ids=true, to_apply=%region_1.3 | all-reduce | flops 1024 | bytes 8192 | tf_op jit(solution)/shard_map/psum | solution.py:90
  332.9 3.4 all_gather.19
  343.3 6.0 %psum.29 = f32[1,2,512]{2,1,0:T(2,128)S(1)} all-reduce(f32[1,2,512]{2,1,0:T(2,128)S(1)} %pad_maximum_fusion.1), channel_id=1, replica_groups=mesh['freq'=32,'tm'=4,'grp'=2] {'tm'}, use_global_device_ids=true, to_apply=%region_3.5 | all-reduce | flops 1024 | bytes 8192 | tf_op jit(solution)/shard_map/psum | solution.py:90
  350.0 3.2 all_gather.20
  356.0 7.4 %psum.30 = f32[1,2,512]{2,1,0:T(2,128)S(1)} all-reduce(f32[1,2,512]{2,1,0:T(2,128)S(1)} %pad_maximum_fusion.2), channel_id=1, replica_groups=mesh['freq'=32,'tm'=4,'grp'=2] {'tm'}, use_global_device_ids=true, to_apply=%region_5.7 | all-reduce | flops 1024 | bytes 8192 | tf_op jit(solution)/shard_map/psum | solution.py:90
  364.1 3.4 all_gather.21
  370.4 6.0 %psum.31 = f32[1,2,512]{2,1,0:T(2,128)S(1)} all-reduce(f32[1,2,512]{2,1,0:T(2,128)S(1)} %pad_maximum_fusion.3), channel_id=1, replica_groups=mesh['freq'=32,'tm'=4,'grp'=2] {'tm'}, use_global_device_ids=true, to_apply=%region_7.9 | all-reduce | flops 1024 | bytes 8192 | tf_op jit(solution)/shard_map/psum | solution.py:90
  377.1 3.2 all_gather.22
  380.3 52.9 %all_gather.23 = f32[32,2,1024]{2,1,0:T(2,128)S(1)} all-gather(f32[1,2,1024]{2,1,0:T(2,128)S(1)} %all_gather.22), channel_id=1, replica_groups=mesh['freq'=32,'tm'=4,'grp'=2] {'freq'}, dimensions={0}, use_global_device_ids=true | all-gather | bytes 270336 | tf_op jit(solution)/shard_map/all_gather | solution.py:94
  434.5 4.6 %fusion.8 = bf16[1,2,2,128,1024]{4,3,2,1,0:T(8,128)(2,1)} fusion(bf16[2,1,128,2,512]{4,2,3,1,0:T(8,128)(2,1)S(1)} %get-tuple-element.17, bf16[2,1,128,2,512]{4,2,3,1,0:T(8,128)(2,1)S(1)} %get-tuple-element.16, bf16[2,2,512,1024]{3,2,1,0:T(8,128)(2,1)} %bitcast.169, bf16[2,512]{1,0:T(2,128)(2,1)S(1)} %convert_element_type.50), kind=kOutput, calls=%fused_computation.19 | convolution fusion | flops 1076887552 | bytes 6293504 | tf_op jit(solution)/shard_map/cpobrq,crpqt->cpobt/dot_general | solution.py:106
  (90 shorter events, 29.3 us)
Async XLA Ops:
  7.2 88.2 %copy-start = (s32[512]{0:T(512)S(1)}, s32[512]{0:T(512)}, u32[]{:S(2)}) copy-start(s32[512]{0:T(512)} %param.12) | copy-start | bytes 6148
  7.2 68.3 %all-gather.2.cloned.1.call-start = ((), (), s32[]{:S(2)}) async-start(), calls=%async_computation.3 | async-start | bytes 6291456 | tf_op jit(solution)/shard_map/all_gather | solution.py:60
  85.1 10.2 %copy-start.3 = (s32[512]{0:T(512)S(1)}, s32[512]{0:T(512)}, u32[]{:S(2)}) copy-start(s32[512]{0:T(512)} %param.13) | copy-start | bytes 6148
  85.1 106.3 %all-to-all-start = ((bf16[32,2,32,1024]{3,2,1,0:T(8,128)(2,1)}), bf16[32,2,32,1024]{3,2,1,0:T(8,128)(2,1)}, u32[]{:S(2)}, u32[]{:S(2)}) async-start(bf16[32,2,32,1024]{3,2,1,0:T(8,128)(2,1)} %broadcast_select_fusion.1), calls=%async_computation | async-start | bytes 8388608 | tf_op jit(solution)/shard_map/all_to_all | solution.py:64
  95.2 222.7 %reduce-scatter.2.cloned.1.call-start = ((), (), s32[]{:S(2)}) async-start(), calls=%async_computation.4 | async-start | bytes 5242880 | tf_op jit(solution)/shard_map/reduce_scatter | solution.py:80
  209.4 7.5 %copy-start.6 = (s32[32]{0:T(128)S(1)}, s32[32]{0:T(128)}, u32[]{:S(2)}) copy-start(s32[32]{0:T(128)} %param.17) | copy-start | bytes 388
  209.4 8.1 %copy-start.5 = (f32[2,512]{1,0:T(2,128)S(1)}, f32[2,512]{1,0:T(2,128)}, u32[]{:S(2)}) copy-start(f32[2,512]{1,0:T(2,128)} %param.14) | copy-start | bytes 12292
  209.4 9.9 %copy-start.2 = (f32[1,2,1024]{2,1,0:T(2,128)S(1)}, f32[1,2,1024]{2,1,0:T(2,128)}, u32[]{:S(2)}) copy-start(f32[1,2,1024]{2,1,0:T(2,128)} %param.11) | copy-start | bytes 24580
  209.4 11.2 %copy-start.7 = (s32[2,256]{1,0:T(2,128)S(1)}, s32[2,256]{1,0:T(2,128)}, u32[]{:S(2)}) copy-start(s32[2,256]{1,0:T(2,128)} %param.15) | copy-start | bytes 6148
  209.4 103.6 %all-to-all-start.1 = ((bf16[32,2,32,1024]{3,2,1,0:T(8,128)(2,1)}), bf16[32,2,32,1024]{3,2,1,0:T(8,128)(2,1)}, u32[]{:S(2)}, u32[]{:S(2)}) async-start(bf16[32,2,32,1024]{3,2,1,0:T(8,128)(2,1)} %broadcast_select_fusion), calls=%async_computation.2 | async-start | bytes 8388608 | tf_op jit(solution)/shard_map/all_to_all | solution.py:65
  317.9 35.8 %copy-start.1 = (f32[1,2,512,256]{3,2,1,0:T(8,128)S(1)}, f32[1,2,512,256]{3,2,1,0:T(8,128)}, u32[]{:S(2)}) copy-start(f32[1,2,512,256]{3,2,1,0:T(8,128)} %reduce-scatter.2.cloned.1.call-done) | copy-start | bytes 3145732
  319.6 113.6 %copy-start.4 = (s32[32]{0:T(128)S(1)}, s32[32]{0:T(128)}, u32[]{:S(2)}) copy-start(s32[32]{0:T(128)} %param.16) | copy-start | bytes 388
Sparse Core Ops, SparseCore 0:
  9.8 65.6 all-gather.1
  204.8 47.6 reduce-scatter.1
where the time goes:
time: 448 us; the launch traced here: 446 us
  waiting for transfers between devices  245 us (55%)
  blocking collectives  94 us (21%)
  matrix products  28.9 us (6%)
  local copies, waits for them, and re-layouts  24.8 us (6%)
  other arithmetic  18.4 us (4%)
  starting transfers between devices  17.7 us (4%)
  between operations  17.6 us (4%)
    all_to_all x1, waiting for transfers between devices, body(): lax.all_to_all(beam_source, 'freq', split_axis=0, concat_axis=2, tiled=True)  90.9 us
    all_to_all x1, waiting for transfers between devices, body(): lax.all_to_all(corr_source, 'freq', split_axis=0, concat_axis=2, tiled=True)  87.4 us
    all_gather x1, waiting for transfers between devices, body(): paired = lax.all_gather(voltages, 'grp', axis=2, tiled=True)  66.2 us
    all_gather x1, blocking collectives, body(): all_gains = lax.all_gather(gains, 'freq', axis=0, tiled=True)  52.9 us
    psum x4, blocking collectives, body(): update = lax.psum(update, 'tm')  27.9 us
    all_gather x4, blocking collectives, body(): gains = lax.all_gather(fresh, 'grp', axis=2, tiled=True)  13.2 us
    all_to_all x1, starting transfers between devices, body(): lax.all_to_all(corr_source, 'freq', split_axis=0, concat_axis=2, tiled=True)  10.2 us
  transfers between devices with their start and end apart: 4, of which 3 were waited for; matrix products, arithmetic and copies ran while one was open for 5% of the time, Pallas kernels for 0%

commit v1 on v0

--- a/solution.py
+++ b/solution.py
@@ -62,7 +62,12 @@
     beam_source = jnp.take(paired, beam_channels, axis=0)
     corr_volts, beam_volts = (
         lax.all_to_all(corr_source, "freq", split_axis=0, concat_axis=2, tiled=True),
-        lax.all_to_all(beam_source, "freq", split_axis=0, concat_axis=2, tiled=True),
+        jnp.concatenate(
+            lax.all_to_all(
+                jnp.stack(jnp.split(beam_source, lax.axis_size("freq"), axis=0)), "freq", 0, 0
+            ),
+            axis=2,
+        ),
     )
     slot_keep = 1 - jnp.take(station_flags, ingest_map)
     keep = jnp.concatenate([slot_keep, slot_keep]).astype(jnp.bfloat16)

time: 448 us -> 446 us (level)
  local copies, waits for them, and re-layouts: 24.8 us -> 48.2 us
  waiting for transfers between devices: 245 us -> 222 us
    all_to_all x1, waiting for transfers between devices: 87.4 us -> 64.4 us  [body(): lax.all_to_all(corr_source, 'freq', split_axis=0, concat_axis=2, tiled=True)]
    unnamed x19 -> x54, local copies, waits for them, and re-layouts: 0.8 us -> 22.6 us
    reshape x0 -> x1, local copies, waits for them, and re-layouts: none -> 4.97 us  [body(): jnp.concatenate(lax.all_to_all(jnp.stack(jnp.split(beam_source, lax.axis_...]
    all_to_all x1 -> x0, local copies, waits for them, and re-layouts: 4.97 us -> none  [body(): lax.all_to_all(beam_source, 'freq', split_axis=0, concat_axis=2, tiled=True)]
  transfers between devices with their start and end apart: 4 -> 4, of which waited for: 3 -> 3; matrix products, arithmetic and copies ran while one was open for 5% -> 10% of each run, Pallas kernels for 0% -> 0%
where the time goes in v1:
time: 446 us; the launch traced here: 445 us
  waiting for transfers between devices  222 us (50%)
  blocking collectives  93.8 us (21%)
  local copies, waits for them, and re-layouts  48.2 us (11%)
  matrix products  28.9 us (6%)
  starting transfers between devices  17.7 us (4%)
  between operations  17.7 us (4%)
  other arithmetic  16.4 us (4%)
    all_to_all x1, waiting for transfers between devices, body(): lax.all_to_all(jnp.stack(jnp.split(beam_source, lax.axis_size('freq'), ax...  90.9 us
    all_gather x1, waiting for transfers between devices, body(): paired = lax.all_gather(voltages, 'grp', axis=2, tiled=True)  66.2 us
    all_to_all x1, waiting for transfers between devices, body(): lax.all_to_all(corr_source, 'freq', split_axis=0, concat_axis=2, tiled=True)  64.4 us
    all_gather x1, blocking collectives, body(): all_gains = lax.all_gather(gains, 'freq', axis=0, tiled=True)  52.9 us
    psum x4, blocking collectives, body(): update = lax.psum(update, 'tm')  27.9 us
    unnamed x54, local copies, waits for them, and re-layouts  22.6 us
    all_gather x4, blocking collectives, body(): gains = lax.all_gather(fresh, 'grp', axis=2, tiled=True)  13 us
    all_to_all x1, starting transfers between devices, body(): lax.all_to_all(corr_source, 'freq', split_axis=0, concat_axis=2, tiled=True)  10.2 us
  transfers between devices with their start and end apart: 4, of which 3 were waited for; matrix products, arithmetic and copies ran while one was open for 10% of the time, Pallas kernels for 0%

profile of v1, /device:TPU:1, one launch (start us, length us, event | category | flops | bytes accessed | tf_op | source)
XLA Modules:
  0.0 444.9 jit_solution(367060601091566179)
XLA Ops:
  9.3 66.2 %all-gather.2.cloned.1.call-done = bf16[32,2,32,1024]{3,2,1,0:T(8,128)(2,1)} async-done(((bf16[32,2,16,1024]{3,2,1,0:T(8,128)(2,1)}), bf16[32,2,32,1024]{3,2,1,0:T(8,128)(2,1)}) %all-gather.2.cloned.1.call-update) | async-done | bytes 4194320 | tf_op jit(solution)/shard_map/all_gather | solution.py:60
  75.5 5.0 %gather_fusion.2 = bf16[32,2,32,1024]{3,2,1,0:T(8,128)(2,1)} fusion(bf16[32,2,32,1024]{3,2,1,0:T(8,128)(2,1)} %all-gather.2.cloned.1.call-done, s32[1024]{0:T(1024)S(1)} %pad_clamp_fusion.2), kind=kCustom, calls=%fused_computation.clone | custom fusion | bytes 8388736 | tf_op jit(solution)/shard_map/jit(_take)/gather | solution.py:61
  80.4 4.6 %broadcast_select_fusion.1 = bf16[32,2,32,1024]{3,2,1,0:T(8,128)(2,1)} fusion(bf16[32,2,32,1024]{3,2,1,0:T(8,128)(2,1)} %gather_fusion.2, pred[32]{0:T(512)(128)(4,1)S(1)} %get-tuple-element.27), kind=kLoop, calls=%fused_computation.14 | loop fusion | flops 2097152 | bytes 8388640 | tf_op jit(solution)/shard_map/jit(_take)/select_n | solution.py:61
  85.1 10.2 %all-to-all-start = ((bf16[32,2,32,1024]{3,2,1,0:T(8,128)(2,1)}), bf16[32,2,32,1024]{3,2,1,0:T(8,128)(2,1)}, u32[]{:S(2)}, u32[]{:S(2)}) async-start(bf16[32,2,32,1024]{3,2,1,0:T(8,128)(2,1)} %broadcast_select_fusion.1), calls=%async_computation | async-start | bytes 8388608 | tf_op jit(solution)/shard_map/all_to_all | solution.py:64
  95.3 3.5 gather_fusion
  99.1 5.0 %gather_fusion.3 = bf16[32,2,32,1024]{3,2,1,0:T(8,128)(2,1)} fusion(bf16[32,2,32,1024]{3,2,1,0:T(8,128)(2,1)} %all-gather.2.cloned.1.call-done, s32[1024]{0:T(1024)S(1)} %pad_clamp_fusion), kind=kCustom, calls=%fused_computation.1.clone | custom fusion | bytes 8388736 | tf_op jit(solution)/shard_map/jit(_take)/gather | solution.py:62
  104.1 2.6 broadcast_select_fusion
  127.0 64.4 %all-to-all-done = bf16[32,2,32,1024]{3,2,1,0:T(8,128)(2,1)} async-done(((bf16[32,2,32,1024]{3,2,1,0:T(8,128)(2,1)}), bf16[32,2,32,1024]{3,2,1,0:T(8,128)(2,1)}, u32[]{:S(2)}, u32[]{:S(2)}) %all-to-all-start) | async-done | bytes 4194336 | tf_op jit(solution)/shard_map/all_to_all | solution.py:64
  191.4 2.6 copy.54
  194.9 2.5 broadcast_multiply_fusion
  198.6 6.2 %fusion.5 = f32[1,2,512,1024]{3,2,1,0:T(8,128)} fusion(bf16[2,1024,1024,1]{2,1,0,3:T(8,128)(2,1)S(1)} %bitcast.296, bf16[1,1,2,512,1024]{4,3,2,1,0:T(8,128)(2,1)S(1)} %maximum_bitcast_fusion.4, bf16[1,1,2,512,1024]{4,3,2,1,0:T(8,128)(2,1)S(1)} %fusion.108), kind=kOutput, calls=%fused_computation.11 | convolution fusion | flops 4298113024 | bytes 12582912 | tf_op jit(solution)/shard_map/corit,crjt->coij/dot_general | solution.py:80
  207.9 7.4 %all-to-all-start.1 = ((bf16[32,1,2,32,1024]{4,3,2,1,0:T(8,128)(2,1)}), bf16[32,1,2,32,1024]{4,3,2,1,0:T(8,128)(2,1)}, u32[]{:S(2)}, u32[]{:S(2)}) async-start(bf16[32,1,2,32,1024]{4,3,2,1,0:T(8,128)(2,1)} %fusion.35), calls=%async_computation.2 | async-start | bytes 8388608 | tf_op jit(solution)/shard_map/all_to_all | solution.py:66
  220.6 90.9 %all-to-all-done.1 = bf16[32,1,2,32,1024]{4,3,2,1,0:T(8,128)(2,1)} async-done(((bf16[32,1,2,32,1024]{4,3,2,1,0:T(8,128)(2,1)}), bf16[32,1,2,32,1024]{4,3,2,1,0:T(8,128)(2,1)}, u32[]{:S(2)}, u32[]{:S(2)}) %all-to-all-start.1) | async-done | bytes 4194336 | tf_op jit(solution)/shard_map/all_to_all | solution.py:66
  311.5 5.0 %copy.58 = bf16[1,2,32,32,1024]{4,3,2,1,0:T(8,128)(2,1)} copy(bf16[1,2,32,32,1024]{4,3,1,0,2:T(8,128)(2,1)} %bitcast.105) | data formatting | bytes 8388608 | tf_op jit(solution)/shard_map/reshape | solution.py:65
  323.0 8.4 %psum.28 = f32[1,2,512]{2,1,0:T(2,128)S(1)} all-reduce(f32[1,2,512]{2,1,0:T(2,128)S(1)} %pad_maximum_fusion), channel_id=1, replica_groups=mesh['freq'=32,'tm'=4,'grp'=2] {'tm'}, use_global_device_ids=true, to_apply=%region_1.3 | all-reduce | flops 1024 | bytes 8192 | tf_op jit(solution)/shard_map/psum | solution.py:95
  331.4 3.2 all_gather.19
  341.6 6.0 %psum.29 = f32[1,2,512]{2,1,0:T(2,128)S(1)} all-reduce(f32[1,2,512]{2,1,0:T(2,128)S(1)} %pad_maximum_fusion.1), channel_id=1, replica_groups=mesh['freq'=32,'tm'=4,'grp'=2] {'tm'}, use_global_device_ids=true, to_apply=%region_3.5 | all-reduce | flops 1024 | bytes 8192 | tf_op jit(solution)/shard_map/psum | solution.py:95
  348.3 3.2 all_gather.20
  354.4 7.4 %psum.30 = f32[1,2,512]{2,1,0:T(2,128)S(1)} all-reduce(f32[1,2,512]{2,1,0:T(2,128)S(1)} %pad_maximum_fusion.2), channel_id=1, replica_groups=mesh['freq'=32,'tm'=4,'grp'=2] {'tm'}, use_global_device_ids=true, to_apply=%region_5.7 | all-reduce | flops 1024 | bytes 8192 | tf_op jit(solution)/shard_map/psum | solution.py:95
  362.5 3.4 all_gather.21
  368.7 6.0 %psum.31 = f32[1,2,512]{2,1,0:T(2,128)S(1)} all-reduce(f32[1,2,512]{2,1,0:T(2,128)S(1)} %pad_maximum_fusion.3), channel_id=1, replica_groups=mesh['freq'=32,'tm'=4,'grp'=2] {'tm'}, use_global_device_ids=true, to_apply=%region_7.9 | all-reduce | flops 1024 | bytes 8192 | tf_op jit(solution)/shard_map/psum | solution.py:95
  375.4 3.2 all_gather.22
  378.6 52.9 %all_gather.23 = f32[32,2,1024]{2,1,0:T(2,128)S(1)} all-gather(f32[1,2,1024]{2,1,0:T(2,128)S(1)} %all_gather.22), channel_id=1, replica_groups=mesh['freq'=32,'tm'=4,'grp'=2] {'freq'}, dimensions={0}, use_global_device_ids=true | all-gather | bytes 270336 | tf_op jit(solution)/shard_map/all_gather | solution.py:99
  432.9 4.6 %fusion.8 = bf16[1,2,2,128,1024]{4,3,2,1,0:T(8,128)(2,1)} fusion(bf16[2,1,128,2,512]{4,2,3,1,0:T(8,128)(2,1)S(1)} %get-tuple-element.17, bf16[2,1,128,2,512]{4,2,3,1,0:T(8,128)(2,1)S(1)} %get-tuple-element.16, bf16[2,2,512,1024]{3,2,1,0:T(8,128)(2,1)} %bitcast.295, bf16[2,512]{1,0:T(2,128)(2,1)S(1)} %convert_element_type.50), kind=kOutput, calls=%fused_computation.19 | convolution fusion | flops 1076887552 | bytes 6293504 | tf_op jit(solution)/shard_map/cpobrq,crpqt->cpobt/dot_general | solution.py:111
  (126 shorter events, 52.7 us)
Async XLA Ops:
  7.2 88.2 %copy-start = (s32[512]{0:T(512)S(1)}, s32[512]{0:T(512)}, u32[]{:S(2)}) copy-start(s32[512]{0:T(512)} %param.12) | copy-start | bytes 6148
  7.2 68.3 %all-gather.2.cloned.1.call-start = ((), (), s32[]{:S(2)}) async-start(), calls=%async_computation.3 | async-start | bytes 6291456 | tf_op jit(solution)/shard_map/all_gather | solution.py:60
  85.1 10.2 %copy-start.5 = (s32[512]{0:T(512)S(1)}, s32[512]{0:T(512)}, u32[]{:S(2)}) copy-start(s32[512]{0:T(512)} %param.13) | copy-start | bytes 6148
  85.1 106.4 %all-to-all-start = ((bf16[32,2,32,1024]{3,2,1,0:T(8,128)(2,1)}), bf16[32,2,32,1024]{3,2,1,0:T(8,128)(2,1)}, u32[]{:S(2)}, u32[]{:S(2)}) async-start(bf16[32,2,32,1024]{3,2,1,0:T(8,128)(2,1)} %broadcast_select_fusion.1), calls=%async_computation | async-start | bytes 8388608 | tf_op jit(solution)/shard_map/all_to_all | solution.py:64
  95.2 221.2 %reduce-scatter.2.cloned.1.call-start = ((), (), s32[]{:S(2)}) async-start(), calls=%async_computation.4 | async-start | bytes 5242880 | tf_op jit(solution)/shard_map/reduce_scatter | solution.py:85
  106.7 19.6 %copy-start.3 = (bf16[32,2,32,1024]{3,2,1,0:T(8,128)(2,1)}, bf16[32,2,32,1024]{3,2,1,0:T(8,128)(2,1)S(1)}, u32[]{:S(2)}) copy-start(bf16[32,2,32,1024]{3,2,1,0:T(8,128)(2,1)S(1)} %broadcast_select_fusion) | copy-start | bytes 12582916
  207.9 7.5 %copy-start.8 = (s32[32]{0:T(128)S(1)}, s32[32]{0:T(128)}, u32[]{:S(2)}) copy-start(s32[32]{0:T(128)} %param.17) | copy-start | bytes 388
  207.9 8.1 %copy-start.7 = (f32[2,512]{1,0:T(2,128)S(1)}, f32[2,512]{1,0:T(2,128)}, u32[]{:S(2)}) copy-start(f32[2,512]{1,0:T(2,128)} %param.14) | copy-start | bytes 12292
  207.9 9.9 %copy-start.4 = (f32[1,2,1024]{2,1,0:T(2,128)S(1)}, f32[1,2,1024]{2,1,0:T(2,128)}, u32[]{:S(2)}) copy-start(f32[1,2,1024]{2,1,0:T(2,128)} %param.11) | copy-start | bytes 24580
  207.9 11.2 %copy-start.9 = (s32[2,256]{1,0:T(2,128)S(1)}, s32[2,256]{1,0:T(2,128)}, u32[]{:S(2)}) copy-start(s32[2,256]{1,0:T(2,128)} %param.15) | copy-start | bytes 6148
  207.9 103.6 %all-to-all-start.1 = ((bf16[32,1,2,32,1024]{4,3,2,1,0:T(8,128)(2,1)}), bf16[32,1,2,32,1024]{4,3,2,1,0:T(8,128)(2,1)}, u32[]{:S(2)}, u32[]{:S(2)}) async-start(bf16[32,1,2,32,1024]{4,3,2,1,0:T(8,128)(2,1)} %fusion.35), calls=%async_computation.2 | async-start | bytes 8388608 | tf_op jit(solution)/shard_map/all_to_all | solution.py:66
  316.5 35.7 %copy-start.2 = (f32[1,2,512,256]{3,2,1,0:T(8,128)S(1)}, f32[1,2,512,256]{3,2,1,0:T(8,128)}, u32[]{:S(2)}) copy-start(f32[1,2,512,256]{3,2,1,0:T(8,128)} %reduce-scatter.2.cloned.1.call-done) | copy-start | bytes 3145732
  318.1 113.4 %copy-start.6 = (s32[32]{0:T(128)S(1)}, s32[32]{0:T(128)}, u32[]{:S(2)}) copy-start(s32[32]{0:T(128)} %param.16) | copy-start | bytes 388
  432.8 5.2 %copy-start.1 = (s32[512]{0:T(512)S(1)}, s32[512]{0:T(512)}, u32[]{:S(2)}) copy-start(s32[512]{0:T(512)} %param.12) | copy-start | bytes 6148
Sparse Core Ops, SparseCore 0:
  9.8 65.6 all-gather.1
  204.9 47.6 reduce-scatter.1
